TPU v7x, 512 devices: a whole 4x4x16 slice. The times are simulated.
512 devices in a mesh: theta: 64 (over z, y_hi, core), gz: 8 (over x, y_lo).
Axes of the slice: x: 4, y: 4 (y_hi: 2, y_lo: 2; y = y_hi * 2 + y_lo), z: 16, core: 2. Of those that a mesh axis runs over, the one named last changes fastest.
Arguments:
- fluid_state: float32 [8, 64, 1024, 128], P(None, 'gz', 'theta'), may hold values from -5 to 20, as said below
- levels: int32 [4, 128], P(None, 'theta'), may hold values from 0 to 1, as said below
- fine_rim: float32 [512, 2, 8, 1024], P('theta', None, None, 'gz'), may hold values from -1.5 to 3, as said below
- slot_owner: int32 [512], replicated, may hold values from 0 to 63, as said below
- slot_block: int32 [512], replicated, may hold values from 0 to 1
- slot_count: int32 [64], replicated, may hold values from 0 to 8, as said below
Outputs:
- residual: float32 [8, 64, 1024, 128], P(None, 'gz', 'theta')
- flux_mismatch: float32 [8, 64, 1024], P(None, 'gz', 'theta')
- inner_flux: float32 [8, 64, 1024], P(None, 'gz', 'theta')
Inputs may be any that keep to these rules, and one draw needn't show every extreme that they name: `fluid_state`: density and pressure are positive; velocities and fields up to 1.5 in magnitude. `fine_rim`: primitive variables: density and pressure positive, velocity and field components up to 1.5 in magnitude. `levels`: each column is 1 on its first r blocks and 0 after, with at least one 1 and one 0. `slot_owner`: slot d * 8 + s belongs to theta device d; the valid slots of a device are its first slot_count[d]; values of other slots are arbitrary; every pair of owner and block is named by exactly two valid slots. `slot_count`: some device fills all 8 slots in every draw.
All inputs are finite; a program needn't handle non-finite values.
Results may differ from a plain program's by a relative error of at most 0.0003.
Values sent between devices are 32-bit elements; how exact they have to be, the bound alone decides.
A program may use at most 64 MiB of HBM per device.

v0:
```python
import math
import jax
import jax.numpy as jnp
from jax import lax
from jax.sharding import PartitionSpec as P

BT = 8
BR = 32
GAMMA = 5.0 / 3.0
AXIS_FLIP = (1.0, -1.0, -1.0, 1.0, 1.0, -1.0, -1.0, 1.0)


def extended_2(cells, sides, width, closed):
    for axis, dim in sides:
        count = lax.axis_size(axis)
        ends = count if closed else count - 1
        head = lax.slice_in_dim(cells, 0, width, axis=dim)
        tail = lax.slice_in_dim(cells, cells.shape[dim] - width, cells.shape[dim], axis=dim)
        cells = jnp.concatenate(
            [
                lax.ppermute(tail, axis, [(i, (i + 1) % count) for i in range(ends)]),
                cells,
                lax.ppermute(head, axis, [((i + 1) % count, i) for i in range(ends)]),
            ],
            axis=dim,
        )
    return cells


def from_partner(block, axis, distance):
    count = lax.axis_size(axis)
    route = []
    for low in range(count):
        high = low | 1 << distance
        if high != low and high < count:
            route += [(low, high), (high, low)]
    return lax.ppermute(block, axis, route)


def primitive(conserved):
    density = conserved[0]
    vel_r = conserved[1] / density
    vel_t = conserved[2] / density
    vel_z = conserved[3] / density
    kinetic = 0.5 * density * (vel_r * vel_r + vel_t * vel_t + vel_z * vel_z)
    magnetic = 0.5 * (
        conserved[5] * conserved[5] + conserved[6] * conserved[6] + conserved[7] * conserved[7]
    )
    pressure = (GAMMA - 1.0) * (conserved[4] - kinetic - magnetic)
    return jnp.stack(
        [density, vel_r, vel_t, vel_z, pressure, conserved[5], conserved[6], conserved[7]]
    )


def physical(states, normal):
    density = states[0]
    velocity = (states[1], states[2], states[3])
    pressure = states[4]
    field = (states[5], states[6], states[7])
    vel_n = velocity[normal]
    field_n = field[normal]
    field_sq = field[0] * field[0] + field[1] * field[1] + field[2] * field[2]
    speed_sq = velocity[0] * velocity[0] + velocity[1] * velocity[1] + velocity[2] * velocity[2]
    vel_dot = velocity[0] * field[0] + velocity[1] * field[1] + velocity[2] * field[2]
    total_p = pressure + 0.5 * field_sq
    energy = pressure / (GAMMA - 1.0) + 0.5 * density * speed_sq + 0.5 * field_sq
    conserved = jnp.stack(
        [
            density,
            density * velocity[0],
            density * velocity[1],
            density * velocity[2],
            energy,
            field[0],
            field[1],
            field[2],
        ]
    )
    momentum = [
        density * velocity[component] * vel_n
        - field[component] * field_n
        + (total_p if component == normal else 0.0)
        for component in (0, 1, 2)
    ]
    induction = [
        vel_n * field[component] - field_n * velocity[component] for component in (0, 1, 2)
    ]
    fluxes = jnp.stack(
        [density * vel_n] + momentum + [(energy + total_p) * vel_n - field_n * vel_dot] + induction
    )
    signal = jnp.abs(vel_n) + jnp.sqrt((GAMMA * pressure + field_sq) / density)
    return (conserved, fluxes, signal)


def rusanov(left_state, right_state, normal):
    cons_left, flux_left, signal_left = physical(left_state, normal)
    cons_right, flux_right, signal_right = physical(right_state, normal)
    return 0.5 * (flux_left + flux_right) - 0.5 * jnp.maximum(signal_left, signal_right) * (
        cons_right - cons_left
    )


def minmod(lower_diff, upper_diff):
    return (
        0.5
        * (jnp.sign(lower_diff) + jnp.sign(upper_diff))
        * jnp.minimum(jnp.abs(lower_diff), jnp.abs(upper_diff))
    )


def face_pairs(extended, axis_dim, length):
    middle = lax.slice_in_dim(extended, 1, length + 3, axis=axis_dim)
    behind = lax.slice_in_dim(extended, 0, length + 2, axis=axis_dim)
    beyond = lax.slice_in_dim(extended, 2, length + 4, axis=axis_dim)
    slopes = minmod(middle - behind, beyond - middle)
    left_state = lax.slice_in_dim(middle + 0.5 * slopes, 0, length + 1, axis=axis_dim)
    right_state = lax.slice_in_dim(middle - 0.5 * slopes, 1, length + 2, axis=axis_dim)
    return (left_state, right_state)


def local_residual(conserved, theta_ext, axial_ext, partner_row, dtheta):
    fields, depth_z, width_t, radial = conserved.shape
    states = primitive(conserved)
    theta_states = jnp.concatenate(
        [primitive(theta_ext[:, :, :2]), states, primitive(theta_ext[:, :, -2:])], axis=2
    )
    axial_states = jnp.concatenate(
        [primitive(axial_ext[:, :2]), states, primitive(axial_ext[:, -2:])], axis=1
    )
    flipper = jnp.array(AXIS_FLIP, jnp.float32).reshape(-1, 1, 1)
    across = primitive(partner_row) * flipper
    behind = jnp.concatenate([across[..., None], states[..., :-1]], axis=-1)
    beyond = jnp.concatenate([states[..., 1:], states[..., -1:]], axis=-1)
    slopes = minmod(states - behind, beyond - states)
    left_state = states + 0.5 * slopes
    right_state = jnp.concatenate([(states - 0.5 * slopes)[..., 1:], states[..., -1:]], axis=-1)
    radial_flux = rusanov(left_state, right_state, 0)
    face_radius = jnp.arange(radial, dtype=jnp.float32) + 1.0
    cell_radius = jnp.arange(radial, dtype=jnp.float32) + 0.5
    outward = radial_flux * (face_radius * dtheta)
    inward = jnp.concatenate([jnp.zeros_like(outward[..., :1]), outward[..., :-1]], axis=-1)
    theta_left, theta_right = face_pairs(theta_states, 2, width_t)
    theta_flux = rusanov(theta_left, theta_right, 1)
    axial_left, axial_right = face_pairs(axial_states, 1, depth_z)
    axial_flux = rusanov(axial_left, axial_right, 2)
    residual = (
        inward
        - outward
        - (theta_flux[:, :, 1:] - theta_flux[:, :, :-1])
        - (axial_flux[:, 1:] - axial_flux[:, :-1]) * (cell_radius * dtheta)
    )
    density = states[0]
    vel_r = states[1]
    vel_t = states[2]
    pressure = states[4]
    field_r = states[5]
    field_t = states[6]
    field_sq = states[5] * states[5] + states[6] * states[6] + states[7] * states[7]
    residual = residual.at[1].add(
        dtheta * (density * vel_t * vel_t + pressure + 0.5 * field_sq - field_t * field_t)
    )
    residual = residual.at[2].add(-dtheta * (density * vel_r * vel_t - field_r * field_t))
    residual = residual.at[6].add(dtheta * (vel_r * field_t - vel_t * field_r))
    return (residual, radial_flux)


def reflux(residual, radial_flux, fine_cells, face_index, dtheta):
    radial = residual.shape[-1]
    positions = jnp.arange(radial, dtype=jnp.int32)
    pick_face = (positions[None, :] == (face_index - 1)[:, None]).astype(jnp.float32)
    coarse_face = jnp.sum(radial_flux * pick_face, axis=-1)
    mismatch = fine_cells - coarse_face
    area = face_index.astype(jnp.float32) * dtheta
    correction = area * mismatch
    outer_cell = (positions[None, :] == face_index[:, None]).astype(jnp.float32)
    volume = (jnp.arange(radial, dtype=jnp.float32) + 0.5) * dtheta
    return ((residual + correction[..., None] * outer_cell) / volume, mismatch)


def fine_faces(fine_rim):
    rim_states = jnp.moveaxis(fine_rim, 2, 0)
    flux_out = rusanov(rim_states[:, :, 0], rim_states[:, :, 1], 0)
    fields, slot_total, length = flux_out.shape
    paired = flux_out.reshape(fields, slot_total, length // (2 * BT), BT, 2)
    return 0.25 * jnp.sum(paired, axis=-1)


def body(fluid_state, levels, fine_rim, slot_owner, slot_block, slot_count):
    fields, depth_z, width_t, radial = fluid_state.shape
    devices = lax.axis_size("theta")
    dtheta = 2.0 * math.pi / (width_t * devices)
    theta_pos = lax.axis_index("theta")
    theta_ext = extended_2(fluid_state, (("theta", 2),), 2, True)
    axial_raw = extended_2(fluid_state, (("gz", 1),), 2, False)
    axial_pos = lax.axis_index("gz")
    ghost_shape = (fields, 2, width_t, radial)
    bottom = jnp.where(
        axial_pos == 0, jnp.broadcast_to(fluid_state[:, :1], ghost_shape), axial_raw[:, :2]
    )
    upper_ghost = jnp.where(
        axial_pos == lax.axis_size("gz") - 1,
        jnp.broadcast_to(fluid_state[:, -1:], ghost_shape),
        axial_raw[:, -2:],
    )
    axial_ext = jnp.concatenate([bottom, fluid_state, upper_ghost], axis=1)
    first_row = fluid_state[..., 0].reshape(fields, depth_z * width_t)
    across = from_partner(first_row, "theta", devices.bit_length() - 2)
    partner_row = across.reshape(fields, depth_z, width_t)
    residual, radial_flux = local_residual(fluid_state, theta_ext, axial_ext, partner_row, dtheta)
    partials = fine_faces(fine_rim)
    slot_cap = fine_rim.shape[0]
    live_slots = (jnp.arange(slot_cap, dtype=jnp.int32) < slot_count[theta_pos]).astype(jnp.float32)
    partials = partials * live_slots[None, :, None, None]
    rows_out = jnp.moveaxis(partials, 1, 0).reshape(slot_cap, fields * depth_z * BT)
    blocks_dev = width_t // BT
    chosen = (
        (slot_owner == theta_pos)[None, :]
        & (slot_block[None, :] == jnp.arange(blocks_dev, dtype=jnp.int32)[:, None])
    ).astype(jnp.float32)
    registers = jnp.dot(
        chosen,
        lax.all_gather(rows_out, "theta", axis=0, tiled=True),
        precision=lax.Precision.HIGHEST,
    )
    fine_cells = (
        registers.reshape(blocks_dev, fields, depth_z, BT)
        .transpose(1, 2, 0, 3)
        .reshape(fields, depth_z, width_t)
    )
    face_index = jnp.repeat(BR * jnp.sum(levels, axis=0), BT)
    result, mismatch = reflux(residual, radial_flux, fine_cells, face_index, dtheta)
    return (result, mismatch, radial_flux[..., 0])


def solution(mesh):
    return jax.shard_map(
        body,
        mesh=mesh,
        in_specs=(
            P(None, "gz", "theta", None),
            P(None, "theta"),
            P("theta", None, None, "gz"),
            P(),
            P(),
            P(),
        ),
        out_specs=(P(None, "gz", "theta", None), P(None, "gz", "theta"), P(None, "gz", "theta")),
        check_vma=False,
    )
```

profile of v0, /device:TPU:1, one launch (start us, length us, event | category | flops | bytes accessed | tf_op | source)
XLA Modules:
  0.0 194.4 jit_solution(17062907998773435416)
XLA Ops:
  7.2 1.7 fusion.64
  9.0 1.3 collective-permute-start.4
  10.2 5.3 %collective-permute-start.3 = (f32[8,2,16,128]{3,2,1,0:T(8,128)}, f32[8,2,16,128]{3,2,1,0:T(8,128)}, u32[]{:S(2)}, u32[]{:S(2)}) collective-permute-start(f32[8,2,16,128]{3,2,1,0:T(8,128)} %get-tuple-element.146), channel_id=1, source_target_pairs={{0,1},{1,2},{2,3},{3,4},{4,5},{5,6},{6,7},{8,9},{9,10},{10,11},{11... | collective-permute-start | bytes 393224 | tf_op jit(solution)/shard_map/ppermute | solution.py:21
  15.6 0.6 copy.490
  16.2 8.7 %collective-permute-start.2 = (f32[8,8,2,128]{3,1,2,0:T(8,128)}, f32[8,8,2,128]{3,1,2,0:T(8,128)S(1)}, u32[]{:S(2)}, u32[]{:S(2)}) collective-permute-start(f32[8,8,2,128]{3,1,2,0:T(8,128)} %copy.490), channel_id=1, source_target_pairs={{8,0},{16,8},{24,16},{32,24},{40,32},{48,40},{56,48},{64,56},{72,6... | collective-permute-start | bytes 196616 | tf_op jit(solution)/shard_map/ppermute | solution.py:23
  24.9 0.6 copy.489
  25.6 1.9 collective-permute-start.1
  27.5 0.2 slice_reduce_fusion.1
  27.8 12.9 %collective-permute-start = (f32[8,128]{1,0:T(8,128)S(1)}, f32[8,128]{1,0:T(8,128)S(1)}, u32[]{:S(2)}, u32[]{:S(2)}) collective-permute-start(f32[8,128]{1,0:T(8,128)S(1)} %reshape_squeeze.3), channel_id=1, source_target_pairs={{0,256},{256,0},{8,264},{264,8},{16,272},{272,16},{24,280},{280,24... | collective-permute-start | bytes 12296 | tf_op jit(solution)/shard_map/ppermute | solution.py:37
  40.7 0.1 copy.370
  41.1 0.1 copy.375
  41.5 0.1 copy.382
  42.0 0.1 copy.386
  42.2 0.1 copy.392
  42.4 0.1 copy.422
  42.6 0.1 copy.423
  42.8 0.1 copy.427
  43.0 0.1 copy.430
  43.2 0.1 copy.434
  43.4 0.1 copy.431
  43.6 0.1 copy.438
  44.8 0.2 subtract_reduce_fusion
  45.0 0.1 copy.488
  45.1 0.6 copy-done.11
  45.8 0.6 dynamic_slice.3
  46.4 0.6 compare_select_fusion
  47.0 0.7 copy.487
  47.8 0.6 add_multiply_fusion.6
  48.5 0.1 reduce_sum.27
  48.9 0.5 convert_multiply_fusion
  49.5 0.7 constant_dynamic-update-slice_fusion.1
  50.2 1.0 fusion.62
  51.2 0.5 broadcast_compare_fusion
  51.8 0.5 add_multiply_fusion.5
  52.3 0.2 copy.362
  52.4 0.2 slice.777
  52.7 0.5 broadcast.594
  53.2 0.7 slice_reduce_fusion.2
  54.6 0.6 copy-done.10
  55.2 0.7 broadcast_multiply_fusion.2
  55.9 1.2 copy.359
  57.1 1.6 fusion.61
  58.7 0.3 slice_subtract_fusion.2
  59.1 0.2 multiply_bitcast_fusion.2
  59.6 0.1 constant_dynamic-update-slice_fusion.30
  60.1 0.3 multiply_reduce_fusion
  60.4 0.7 copy-done.4
  61.1 0.8 slice_reduce_fusion
  62.1 0.3 fusion.4
  62.5 0.1 multiply_bitcast_fusion.1
  63.2 0.4 fusion.1
  63.6 0.9 broadcast_select_fusion
  64.7 0.4 fusion.3
  65.2 0.1 multiply_bitcast_fusion
  65.9 0.2 multiply_subtract_fusion
  66.1 0.6 copy-done.5
  66.7 0.3 fusion.7
  66.9 0.6 copy-done.1
  67.7 115.7 %all-gather.2.cloned.1.call-done = f32[512,512]{1,0:T(8,128)} async-done(((f32[8,512]{1,0:T(8,128)}), f32[512,512]{1,0:T(8,128)}) %all-gather.2.cloned.1.call-update) | async-done | bytes 1048592 | tf_op jit(solution)/shard_map/all_gather | solution.py:222
  183.4 1.7 fusion.47
  185.2 0.1 reshape.1788
  185.3 0.6 copy-done.9
  186.0 0.6 broadcast_multiply_fusion.3
  186.6 1.0 add_divide_fusion
  (191 shorter events, 6.1 us)
Async XLA Ops:
  7.2 8.4 %copy-start = (f32[8,8,16,128]{3,2,1,0:T(8,128)S(1)}, f32[8,8,16,128]{3,2,1,0:T(8,128)}, u32[]{:S(2)}) copy-start(f32[8,8,16,128]{3,2,1,0:T(8,128)} %param.13) | copy-start | bytes 1572868
  7.2 176.2 %all-gather.2.cloned.1.call-start = ((), (), s32[]{:S(2)}) async-start(), calls=%async_computation | async-start | bytes 1064960 | tf_op jit(solution)/shard_map/all_gather | solution.py:222
  9.0 54.6 %collective-permute-start.4 = (f32[8,2,16,128]{3,2,1,0:T(8,128)}, f32[8,2,16,128]{3,2,1,0:T(8,128)}, u32[]{:S(2)}, u32[]{:S(2)}) collective-permute-start(f32[8,2,16,128]{3,2,1,0:T(8,128)} %get-tuple-element.147), channel_id=1, source_target_pairs={{1,0},{2,1},{3,2},{4,3},{5,4},{6,5},{7,6},{9,8},{10,9},{11,10},{12... | collective-permute-start | bytes 393224 | tf_op jit(solution)/shard_map/ppermute | solution.py:23
  10.2 54.3 %collective-permute-start.3 = (f32[8,2,16,128]{3,2,1,0:T(8,128)}, f32[8,2,16,128]{3,2,1,0:T(8,128)}, u32[]{:S(2)}, u32[]{:S(2)}) collective-permute-start(f32[8,2,16,128]{3,2,1,0:T(8,128)} %get-tuple-element.146), channel_id=1, source_target_pairs={{0,1},{1,2},{2,3},{3,4},{4,5},{5,6},{6,7},{8,9},{9,10},{10,11},{11... | collective-permute-start | bytes 393224 | tf_op jit(solution)/shard_map/ppermute | solution.py:21
  16.2 45.7 %collective-permute-start.2 = (f32[8,8,2,128]{3,1,2,0:T(8,128)}, f32[8,8,2,128]{3,1,2,0:T(8,128)S(1)}, u32[]{:S(2)}, u32[]{:S(2)}) collective-permute-start(f32[8,8,2,128]{3,1,2,0:T(8,128)} %copy.490), channel_id=1, source_target_pairs={{8,0},{16,8},{24,16},{32,24},{40,32},{48,40},{56,48},{64,56},{72,6... | collective-permute-start | bytes 196616 | tf_op jit(solution)/shard_map/ppermute | solution.py:23
  25.6 36.4 %collective-permute-start.1 = (f32[8,8,2,128]{3,1,2,0:T(8,128)}, f32[8,8,2,128]{3,1,2,0:T(8,128)S(1)}, u32[]{:S(2)}, u32[]{:S(2)}) collective-permute-start(f32[8,8,2,128]{3,1,2,0:T(8,128)} %copy.489), channel_id=1, source_target_pairs={{0,8},{8,16},{16,24},{24,32},{32,40},{40,48},{48,56},{56,64},{64,7... | collective-permute-start | bytes 196616 | tf_op jit(solution)/shard_map/ppermute | solution.py:21
  27.5 13.2 %copy-start.2 = (f32[8,2,8,128]{3,2,1,0:T(8,128)S(1)}, f32[8,2,8,128]{3,2,1,0:T(8,128)}, u32[]{:S(2)}) copy-start(f32[8,2,8,128]{3,2,1,0:T(8,128)} %param.15) | copy-start | bytes 196612
  27.8 24.9 %collective-permute-start = (f32[8,128]{1,0:T(8,128)S(1)}, f32[8,128]{1,0:T(8,128)S(1)}, u32[]{:S(2)}, u32[]{:S(2)}) collective-permute-start(f32[8,128]{1,0:T(8,128)S(1)} %reshape_squeeze.3), channel_id=1, source_target_pairs={{0,256},{256,0},{8,264},{264,8},{16,272},{272,16},{24,280},{280,24... | collective-permute-start | bytes 12296 | tf_op jit(solution)/shard_map/ppermute | solution.py:37
  45.1 0.7 copy-start.11
  47.8 0.7 copy-start.8
  50.2 1.0 copy-start.7
  54.6 0.7 copy-start.10
  60.4 0.7 copy-start.4
  66.1 0.6 copy-start.5
  66.7 0.8 copy-start.1
  67.6 115.8 %copy-start.3 = (s32[512]{0:T(512)S(1)}, s32[512]{0:T(512)}, u32[]{:S(2)}) copy-start(s32[512]{0:T(512)} %param.17) | copy-start | bytes 6148
  67.6 115.8 %copy-start.6 = (pred[512]{0:T(512)(128)(4,1)S(1)}, pred[512]{0:T(512)(128)(4,1)}, u32[]{:S(2)}) copy-start(pred[512]{0:T(512)(128)(4,1)} %broadcast_compare_fusion) | copy-start | bytes 1540
  185.3 0.6 copy-start.9
Sparse Core Ops, SparseCore 0:
  47.9 135.4 all-gather.1
where the time goes:
time: 195 us; the launch traced here: 194 us
  waiting for transfers between devices  116 us (59%)
  starting transfers between devices  30.1 us (15%)
  local copies, waits for them, and re-layouts  17.2 us (9%)
  between operations  15.3 us (8%)
  other arithmetic  14.4 us (7%)
    all_gather x1, waiting for transfers between devices, body(): lax.all_gather(rows_out, 'theta', axis=0, tiled=True)  116 us
    ppermute x1, starting transfers between devices, from_partner(): return lax.ppermute(block, axis, route)  12.9 us
    ppermute x2, starting transfers between devices, extended_2(): lax.ppermute(head, axis, [((i + 1) % count, i) for i in range(ends)])  9.94 us
    ppermute x2, starting transfers between devices, extended_2(): lax.ppermute(tail, axis, [(i, (i + 1) % count) for i in range(ends)])  7.23 us
    unnamed x45, local copies, waits for them, and re-layouts  5.39 us
  transfers between devices with their start and end apart: 6, of which 1 were waited for; matrix products, arithmetic and copies ran while one was open for 12% of the time, Pallas kernels for 0%

commit v1 on v0

--- a/solution.py
+++ b/solution.py
@@ -219,7 +219,9 @@
     ).astype(jnp.float32)
     registers = jnp.dot(
         chosen,
-        lax.all_gather(rows_out, "theta", axis=0, tiled=True),
+        jnp.concatenate(
+            lax.all_to_all(jnp.stack([rows_out] * lax.axis_size("theta")), "theta", 0, 0), axis=0
+        ),
         precision=lax.Precision.HIGHEST,
     )
     fine_cells = (

time: 195 us -> 115 us (0.59)
  waiting for transfers between devices: 116 us -> 13 us
  local copies, waits for them, and re-layouts: 17.2 us -> 35.9 us
  between operations: 15.3 us -> 1.85 us
  starting transfers between devices: 30.1 us -> 39.7 us
  other arithmetic: 14.4 us -> 19 us
    all_gather x1 -> x0, waiting for transfers between devices: 116 us -> none  [body(): lax.all_gather(rows_out, 'theta', axis=0, tiled=True)]
    all_to_all x0 -> x1, waiting for transfers between devices: none -> 12.9 us  [body(): lax.all_to_all(jnp.stack([rows_out] * lax.axis_size('theta')), 'theta', 0...]
    another operation x15, local copies, waits for them, and re-layouts: 0.82 us -> 11.2 us  [primitive(): jnp.stack([density, vel_r, vel_t, vel_z, pressure, conserved[5], conserve...]
    all_to_all x0 -> x1, starting transfers between devices: none -> 9.64 us  [body(): lax.all_to_all(jnp.stack([rows_out] * lax.axis_size('theta')), 'theta', 0...]
    unnamed x45 -> x59, local copies, waits for them, and re-layouts: 5.39 us -> 11.4 us
  transfers between devices with their start and end apart: 6 -> 6, of which waited for: 1 -> 1; matrix products, arithmetic and copies ran while one was open for 12% -> 41% of each run, Pallas kernels for 0% -> 0%
where the time goes in v1:
time: 115 us; the launch traced here: 113 us
  starting transfers between devices  39.7 us (35%)
  local copies, waits for them, and re-layouts  35.9 us (31%)
  other arithmetic  19 us (17%)
  waiting for transfers between devices  13 us (11%)
  matrix products  3.55 us (3%)
  between operations  1.85 us (2%)
    all_to_all x1, waiting for transfers between devices, body(): lax.all_to_all(jnp.stack([rows_out] * lax.axis_size('theta')), 'theta', 0...  12.9 us
    ppermute x1, starting transfers between devices, from_partner(): return lax.ppermute(block, axis, route)  12.9 us
    unnamed x59, local copies, waits for them, and re-layouts  11.4 us
    another operation x15, local copies, waits for them, and re-layouts, primitive(): jnp.stack([density, vel_r, vel_t, vel_z, pressure, conserved[5], conserve...  11.2 us
    ppermute x2, starting transfers between devices, extended_2(): lax.ppermute(head, axis, [((i + 1) % count, i) for i in range(ends)])  9.94 us
    all_to_all x1, starting transfers between devices, body(): lax.all_to_all(jnp.stack([rows_out] * lax.axis_size('theta')), 'theta', 0...  9.64 us
    ppermute x2, starting transfers between devices, extended_2(): lax.ppermute(tail, axis, [(i, (i + 1) % count) for i in range(ends)])  7.24 us
    dot_general x1, matrix products, body(): jnp.dot(chosen, jnp.concatenate(lax.all_to_all(jnp.stack([rows_out] * lax...  3.55 us
  transfers between devices with their start and end apart: 6, of which 1 were waited for; matrix products, arithmetic and copies ran while one was open for 41% of the time, Pallas kernels for 0%

profile of v1, /device:TPU:1, one launch (start us, length us, event | category | flops | bytes accessed | tf_op | source)
XLA Modules:
  0.0 113.0 jit_solution(13623816264367172926)
XLA Ops:
  0.6 1.8 %fusion.64 = (f32[8,2,16,128]{3,2,1,0:T(8,128)}, f32[8,2,16,128]{3,2,1,0:T(8,128)}) fusion(f32[8,8,16,128]{3,2,1,0:T(8,128)} %param.13), kind=kLoop, calls=%fused_computation.363 | loop fusion | bytes 524288 | tf_op jit(solution)/shard_map/slice | solution.py:18
  2.4 1.3 %collective-permute-start.4 = (f32[8,2,16,128]{3,2,1,0:T(8,128)}, f32[8,2,16,128]{3,2,1,0:T(8,128)}, u32[]{:S(2)}, u32[]{:S(2)}) collective-permute-start(f32[8,2,16,128]{3,2,1,0:T(8,128)} %get-tuple-element.147), channel_id=1, source_target_pairs={{1,0},{2,1},{3,2},{4,3},{5,4},{6,5},{7,6},{9,8},{10,9},{11,10},{12... | collective-permute-start | bytes 393224 | tf_op jit(solution)/shard_map/ppermute | solution.py:23
  3.7 5.3 %collective-permute-start.3 = (f32[8,2,16,128]{3,2,1,0:T(8,128)}, f32[8,2,16,128]{3,2,1,0:T(8,128)}, u32[]{:S(2)}, u32[]{:S(2)}) collective-permute-start(f32[8,2,16,128]{3,2,1,0:T(8,128)} %get-tuple-element.146), channel_id=1, source_target_pairs={{0,1},{1,2},{2,3},{3,4},{4,5},{5,6},{6,7},{8,9},{9,10},{10,11},{11... | collective-permute-start | bytes 393224 | tf_op jit(solution)/shard_map/ppermute | solution.py:21
  9.1 0.6 copy.489
  9.7 8.7 %collective-permute-start.2 = (f32[8,8,2,128]{3,1,2,0:T(8,128)}, f32[8,8,2,128]{3,1,2,0:T(8,128)S(1)}, u32[]{:S(2)}, u32[]{:S(2)}) collective-permute-start(f32[8,8,2,128]{3,1,2,0:T(8,128)} %copy.489), channel_id=1, source_target_pairs={{8,0},{16,8},{24,16},{32,24},{40,32},{48,40},{56,48},{64,56},{72,6... | collective-permute-start | bytes 196616 | tf_op jit(solution)/shard_map/ppermute | solution.py:23
  18.4 0.6 copy.488
  19.0 1.9 %collective-permute-start.1 = (f32[8,8,2,128]{3,1,2,0:T(8,128)}, f32[8,8,2,128]{3,1,2,0:T(8,128)S(1)}, u32[]{:S(2)}, u32[]{:S(2)}) collective-permute-start(f32[8,8,2,128]{3,1,2,0:T(8,128)} %copy.488), channel_id=1, source_target_pairs={{0,8},{8,16},{16,24},{24,32},{32,40},{40,48},{48,56},{56,64},{64,7... | collective-permute-start | bytes 196616 | tf_op jit(solution)/shard_map/ppermute | solution.py:21
  20.9 0.2 slice_reduce_fusion.1
  21.1 0.7 reshape_squeeze.3
  21.8 12.9 %collective-permute-start = (f32[8,128]{1,0:T(8,128)}, f32[8,128]{1,0:T(8,128)}, u32[]{:S(2)}, u32[]{:S(2)}) collective-permute-start(f32[8,128]{1,0:T(8,128)} %reshape_squeeze.3), channel_id=1, source_target_pairs={{0,256},{256,0},{8,264},{264,8},{16,272},{272,16},{24,280},{280,24... | collective-permute-start | bytes 12296 | tf_op jit(solution)/shard_map/ppermute | solution.py:37
  38.8 0.2 subtract_reduce_fusion
  39.2 0.6 copy-done.18
  39.8 0.6 dynamic_slice.3
  40.4 0.6 compare_select_fusion
  41.2 1.1 stack.103
  42.3 9.6 %all-to-all-start = ((f32[64,8,512]{2,1,0:T(8,128)}), f32[64,8,512]{2,1,0:T(8,128)S(1)}, u32[]{:S(2)}, u32[]{:S(2)}) async-start(f32[64,8,512]{2,1,0:T(8,128)} %stack.103), calls=%async_computation | async-start | bytes 2097152 | tf_op jit(solution)/shard_map/all_to_all | solution.py:223
  52.0 0.5 add_multiply_fusion.6
  53.0 0.6 convert_multiply_fusion
  53.7 0.7 constant_dynamic-update-slice_fusion.1
  54.5 1.1 fusion.62
  55.6 0.6 broadcast_compare_fusion
  56.2 0.5 add_multiply_fusion.5
  57.1 1.4 %slice_divide_fusion.17 = (f32[1,128]{1,0:T(1,128)}, f32[1,128]{1,0:T(1,128)}, f32[1,128]{1,0:T(1,128)}) fusion(f32[8,128]{1,0:T(8,128)} %collective-permute-done), kind=kLoop, calls=%fused_computation.353 | loop fusion | flops 384 | bytes 3584 | tf_op jit(solution)/shard_map/div | solution.py:42
  58.4 0.5 broadcast.595
  59.0 2.1 %slice_reduce_fusion.2 = (f32[128]{0:T(128)}, f32[128]{0:T(128)}, f32[128]{0:T(128)}, f32[128]{0:T(128)}, f32[128]{0:T(128)}, /*index=5*/f32[128]{0:T(128)}, f32[128]{0:T(128)}, f32[128]{0:T(128)}) fusion(f32[8,128]{1,0:T(8,128)} %collective-permute-done, f32[1,128]{1,0:T(1,128)} %get-tuple-element.198, f32[1,128]{1,0:T(1,128)} %get-tuple-element.199, ...), kind=kLoop, calls=%fused_computation.354 | loop fusion | flops 2048 | bytes 8196 | tf_op jit(solution)/shard_map/slice | solution.py:47
  61.1 1.3 %stack.74 = f32[1,8,16,1]{2,1,3,0:T(8,128)} reshape(f32[128]{0:T(128)} %get-tuple-element.58) | data formatting | bytes 1024 | tf_op jit(solution)/shard_map/stack | solution.py:50
  62.4 1.3 %constant_dynamic-update-slice_fusion.13 = f32[8,8,16,1]{2,1,3,0:T(8,128)} fusion(f32[1,8,16,1]{2,1,3,0:T(8,128)} %stack.74), kind=kLoop, calls=%fused_computation.50 | loop fusion | bytes 4608
  63.7 1.3 %stack.75 = f32[1,8,16,1]{2,1,3,0:T(8,128)} reshape(f32[128]{0:T(128)} %get-tuple-element.59) | data formatting | bytes 1024 | tf_op jit(solution)/shard_map/stack | solution.py:50
  65.0 1.3 %stack.76 = f32[1,8,16,1]{2,1,3,0:T(8,128)} reshape(f32[128]{0:T(128)} %get-tuple-element.60) | data formatting | bytes 1024 | tf_op jit(solution)/shard_map/stack | solution.py:50
  66.3 1.3 %stack.77 = f32[1,8,16,1]{2,1,3,0:T(8,128)} reshape(f32[128]{0:T(128)} %get-tuple-element.61) | data formatting | bytes 1024 | tf_op jit(solution)/shard_map/stack | solution.py:50
  67.6 1.3 %stack.78 = f32[1,8,16,1]{2,1,3,0:T(8,128)} reshape(f32[128]{0:T(128)} %get-tuple-element.57) | data formatting | bytes 1024 | tf_op jit(solution)/shard_map/stack | solution.py:50
  69.0 1.2 %stack.79 = f32[1,8,16,1]{2,1,3,0:T(8,128)} reshape(f32[128]{0:T(128)} %get-tuple-element.56) | data formatting | bytes 1024 | tf_op jit(solution)/shard_map/stack | solution.py:50
  70.2 1.3 %stack.80 = f32[1,8,16,1]{2,1,3,0:T(8,128)} reshape(f32[128]{0:T(128)} %get-tuple-element.55) | data formatting | bytes 1024 | tf_op jit(solution)/shard_map/stack | solution.py:50
  71.5 1.3 %stack.81 = f32[1,8,16,1]{2,1,3,0:T(8,128)} reshape(f32[128]{0:T(128)} %get-tuple-element.54) | data formatting | bytes 1024 | tf_op jit(solution)/shard_map/stack | solution.py:50
  72.8 1.3 %constant_dynamic-update-slice_fusion.12 = f32[8,8,16,1]{2,1,3,0:T(8,128)} fusion(f32[8,8,16,1]{2,1,3,0:T(8,128)} %constant_dynamic-update-slice_fusion.13, f32[1,8,16,1]{2,1,3,0:T(8,128)} %stack.75), kind=kLoop, calls=%fused_computation.49 | loop fusion | bytes 8192
  74.1 0.6 constant_dynamic-update-slice_fusion.11
  74.8 0.6 constant_dynamic-update-slice_fusion.10
  75.4 0.6 constant_dynamic-update-slice_fusion.9
  76.1 0.6 constant_dynamic-update-slice_fusion.8
  76.8 0.6 constant_dynamic-update-slice_fusion.7
  77.5 0.6 constant_dynamic-update-slice_fusion.6
  78.1 1.4 %broadcast_multiply_fusion.2 = f32[8,8,16,1]{2,1,3,0:T(8,128)} fusion(f32[8,8,16,1]{2,1,3,0:T(8,128)} %constant_dynamic-update-slice_fusion.6, f32[8]{0:T(128)S(1)} %copy-done.17), kind=kLoop, calls=%fused_computation.308 | loop fusion | flops 1024 | bytes 8224 | tf_op jit(solution)/shard_map/mul | solution.py:131
  79.6 2.0 %copy.358 = f32[8,8,16,1]{3,2,1,0:T(8,128)} copy(f32[8,8,16,1]{2,1,3,0:T(8,128)} %broadcast_multiply_fusion.2) | data formatting | bytes 8192 | tf_op jit(solution)/shard_map/mul | solution.py:131
  81.6 1.9 %fusion.61 = (f32[8,8,16,128]{3,2,1,0:T(8,128)S(1)}, f32[8,8,16,128]{3,2,1,0:T(8,128)S(1)}) fusion(f32[8,8,16,128]{3,2,1,0:T(8,128)S(1)} %constant_dynamic-update-slice_fusion, f32[8,8,16,1]{3,2,1,0:T(8,128)S(1)} %slice.777, f32[8,8,16,127]{3,2,1,0:T(8,128)} %get-tuple-element.141, f32[8,8,16,127]{3,2,1,0:T(8,128)} %get-tuple-element.140, ...), kind=kLoop, calls=%fused_computation.360 | loop fusion | flops 1835008 | bytes 2621440 | tf_op jit(solution)/shard_map/add | solution.py:135
  83.5 0.3 slice_subtract_fusion.2
  84.9 0.9 multiply_reduce_fusion
  85.8 0.6 copy-done.11
  86.4 0.8 slice_reduce_fusion
  87.4 0.3 fusion.4
  88.5 0.4 fusion.1
  88.9 0.9 broadcast_select_fusion
  90.1 0.4 fusion.3
  91.2 0.2 multiply_subtract_fusion
  91.5 0.6 copy-done.12
  92.1 0.3 fusion.7
  92.4 0.6 copy-done.1
  93.0 12.9 %all-to-all-done = f32[64,8,512]{2,1,0:T(8,128)S(1)} async-done(((f32[64,8,512]{2,1,0:T(8,128)}), f32[64,8,512]{2,1,0:T(8,128)S(1)}, u32[]{:S(2)}, u32[]{:S(2)}) %all-to-all-start) | async-done | bytes 1048608 | tf_op jit(solution)/shard_map/all_to_all | solution.py:223
  106.0 0.3 copy.485
  106.3 0.3 copy-done.10
  106.7 0.3 copy-done.13
  107.0 3.5 %convolution_bitcast_fusion = f32[8,8,2,8]{3,2,1,0:T(2,128)S(1)} fusion(f32[8,8,8,512]{3,2,1,0:T(8,128)S(1)} %bitcast.48, pred[512]{0:T(512)(128)(4,1)S(1)} %copy-done.13, s32[512]{0:T(512)S(1)} %copy-done.10), kind=kOutput, calls=%fused_computation | convolution fusion | flops 6293504 | bytes 1055232 | tf_op jit(solution)/shard_map/dot_general | solution.py:220
  110.7 0.7 copy-done.2
  111.4 0.6 broadcast_multiply_fusion.3
  112.0 1.0 add_divide_fusion
  (204 shorter events, 8.3 us)
Async XLA Ops:
  0.6 8.4 %copy-start = (f32[8,8,16,128]{3,2,1,0:T(8,128)S(1)}, f32[8,8,16,128]{3,2,1,0:T(8,128)}, u32[]{:S(2)}) copy-start(f32[8,8,16,128]{3,2,1,0:T(8,128)} %param.13) | copy-start | bytes 1572868
  2.4 86.5 %collective-permute-start.4 = (f32[8,2,16,128]{3,2,1,0:T(8,128)}, f32[8,2,16,128]{3,2,1,0:T(8,128)}, u32[]{:S(2)}, u32[]{:S(2)}) collective-permute-start(f32[8,2,16,128]{3,2,1,0:T(8,128)} %get-tuple-element.147), channel_id=1, source_target_pairs={{1,0},{2,1},{3,2},{4,3},{5,4},{6,5},{7,6},{9,8},{10,9},{11,10},{12... | collective-permute-start | bytes 393224 | tf_op jit(solution)/shard_map/ppermute | solution.py:23
  3.7 86.3 %collective-permute-start.3 = (f32[8,2,16,128]{3,2,1,0:T(8,128)}, f32[8,2,16,128]{3,2,1,0:T(8,128)}, u32[]{:S(2)}, u32[]{:S(2)}) collective-permute-start(f32[8,2,16,128]{3,2,1,0:T(8,128)} %get-tuple-element.146), channel_id=1, source_target_pairs={{0,1},{1,2},{2,3},{3,4},{4,5},{5,6},{6,7},{8,9},{9,10},{10,11},{11... | collective-permute-start | bytes 393224 | tf_op jit(solution)/shard_map/ppermute | solution.py:21
  9.7 77.5 %collective-permute-start.2 = (f32[8,8,2,128]{3,1,2,0:T(8,128)}, f32[8,8,2,128]{3,1,2,0:T(8,128)S(1)}, u32[]{:S(2)}, u32[]{:S(2)}) collective-permute-start(f32[8,8,2,128]{3,1,2,0:T(8,128)} %copy.489), channel_id=1, source_target_pairs={{8,0},{16,8},{24,16},{32,24},{40,32},{48,40},{56,48},{64,56},{72,6... | collective-permute-start | bytes 196616 | tf_op jit(solution)/shard_map/ppermute | solution.py:23
  19.0 68.3 %collective-permute-start.1 = (f32[8,8,2,128]{3,1,2,0:T(8,128)}, f32[8,8,2,128]{3,1,2,0:T(8,128)S(1)}, u32[]{:S(2)}, u32[]{:S(2)}) collective-permute-start(f32[8,8,2,128]{3,1,2,0:T(8,128)} %copy.488), channel_id=1, source_target_pairs={{0,8},{8,16},{16,24},{24,32},{32,40},{40,48},{48,56},{56,64},{64,7... | collective-permute-start | bytes 196616 | tf_op jit(solution)/shard_map/ppermute | solution.py:21
  20.9 13.8 %copy-start.3 = (f32[8,2,8,128]{3,2,1,0:T(8,128)S(1)}, f32[8,2,8,128]{3,2,1,0:T(8,128)}, u32[]{:S(2)}) copy-start(f32[8,2,8,128]{3,2,1,0:T(8,128)} %param.15) | copy-start | bytes 196612
  21.8 35.3 %collective-permute-start = (f32[8,128]{1,0:T(8,128)}, f32[8,128]{1,0:T(8,128)}, u32[]{:S(2)}, u32[]{:S(2)}) collective-permute-start(f32[8,128]{1,0:T(8,128)} %reshape_squeeze.3), channel_id=1, source_target_pairs={{0,256},{256,0},{8,264},{264,8},{16,272},{272,16},{24,280},{280,24... | collective-permute-start | bytes 12296 | tf_op jit(solution)/shard_map/ppermute | solution.py:37
  39.2 0.7 copy-start.18
  42.3 63.7 %all-to-all-start = ((f32[64,8,512]{2,1,0:T(8,128)}), f32[64,8,512]{2,1,0:T(8,128)S(1)}, u32[]{:S(2)}, u32[]{:S(2)}) async-start(f32[64,8,512]{2,1,0:T(8,128)} %stack.103), calls=%async_computation | async-start | bytes 2097152 | tf_op jit(solution)/shard_map/all_to_all | solution.py:223
  52.0 0.7 copy-start.15
  54.5 1.1 copy-start.14
  72.8 1.3 %copy-start.9 = (f32[1,8,16,1]{2,1,3,0:T(8,128)S(1)}, f32[1,8,16,1]{2,1,3,0:T(8,128)}, u32[]{:S(2)}) copy-start(f32[1,8,16,1]{2,1,3,0:T(8,128)} %stack.76) | copy-start | bytes 1540
  74.1 0.7 copy-start.8
  74.8 0.7 copy-start.7
  75.4 0.7 copy-start.6
  76.1 0.7 copy-start.4
  76.8 0.7 copy-start.5
  77.5 0.7 copy-start.17
  85.8 0.6 copy-start.11
  91.4 0.6 copy-start.12
  92.1 0.8 copy-start.1
  106.0 0.7 copy-start.10
  106.3 0.7 copy-start.13
  110.6 0.8 copy-start.2
  110.7 0.7 copy-start.16
